TPU v7x, 32 devices: a whole 2x2x4 slice. The times are simulated.
32 devices in a mesh: seq: 8 (over y, x, core), tensor: 4 (over z).
Axes of the slice: x: 2, y: 2, z: 4, core: 2. Of those that a mesh axis runs over, the one named last changes fastest.
Arguments:
- patches: bfloat16 [2048, 6144], P('seq', 'tensor'), may hold values from -60 to 60
- segment_ids: int32 [2048], replicated, may hold values from 0 to 3, never falling along the last dimension, each value on 1 to 768 neighbouring positions
- w_query: bfloat16 [6144, 1024], P('seq', 'tensor'), may hold values from -0.078125 to 0.078125
- w_key: bfloat16 [6144, 1024], P('seq', 'tensor'), may hold values from -0.078125 to 0.078125
- w_value: bfloat16 [6144, 1024], P('seq', 'tensor'), may hold values from -0.078125 to 0.078125
- w_out: bfloat16 [1024, 6144], P('seq', 'tensor'), may hold values from -0.1875 to 0.1875
Outputs:
- attended: bfloat16 [2048, 6144], P('seq', 'tensor')
Inputs may be any that keep to these rules, and one draw needn't show every extreme that they name: `segment_ids`: image ids never fall along the row; every image holds at most 768 patches and some image exactly that many.
All inputs are finite; a program needn't handle non-finite values.
Results may differ from a plain program's by a relative error of at most 0.012.
The roundings to bfloat16 on the way count: a program that leaves them out, or rounds other values in their place, can miss the bound.
Values may be sent and summed in bfloat16 or wider, within the bound.
No kernel may reach another device: no remote copies, remote signals or barrier semaphores. Data moves between devices by JAX's collectives and lax.ppermute only.
A program may use at most 64 MiB of HBM per device.

v0:
```python
import jax
import jax.numpy as jnp
from jax import lax
from jax.sharding import PartitionSpec as P

HS = 128
SPAN = 3


def shifted(x, axis, by):
    count = lax.axis_size(axis)
    pairs = [(i, i + by) for i in range(count) if 0 <= i + by < count]
    return lax.ppermute(x, axis, pairs)


def on_device(patches, segment_ids, w_query, w_key, w_value, w_out):
    tok_rows = patches.shape[0]
    col_width = w_query.shape[1]
    local_heads = col_width // HS
    seq_count = lax.axis_size("seq")
    device = lax.axis_index("seq")
    gathered = lax.all_gather(patches, "tensor", axis=1, tiled=True)
    pieces = (
        lax.all_gather(w_query, "seq", axis=0, tiled=True),
        lax.all_gather(w_key, "seq", axis=0, tiled=True),
        lax.all_gather(w_value, "seq", axis=0, tiled=True),
    )
    sums = tuple((jnp.dot(gathered, piece, preferred_element_type=jnp.float32) for piece in pieces))
    queries, keys_here, values_here = [
        item.astype(jnp.bfloat16).reshape(tok_rows, local_heads, HS) for item in sums
    ]

    def source_ids(offset_by):
        source = device - offset_by
        inside = (source >= 0) & (source < seq_count)
        begin = jnp.clip(source, 0, seq_count - 1) * tok_rows
        picked = lax.dynamic_slice_in_dim(segment_ids, begin, tok_rows)
        return jnp.where(inside, picked, -1)

    blocks = [(0, keys_here, values_here)]
    offsets = list(range(1, SPAN + 1)) + [-depth for depth in range(1, SPAN + 1)]
    for offset_by in offsets:
        moved = shifted((keys_here, values_here), "seq", offset_by)
        blocks.append((offset_by, moved[0], moved[1]))
    key_block = jnp.concatenate([entry[1] for entry in blocks], 0)
    value_block = jnp.concatenate([entry[2] for entry in blocks], 0)
    key_ids = jnp.concatenate([source_ids(entry[0]) for entry in blocks], 0)
    own_ids = source_ids(0)
    scaling = HS ** (-0.5)
    scores = (
        jnp.einsum("qhd,khd->hqk", queries, key_block, preferred_element_type=jnp.float32) * scaling
    )
    same_image = (own_ids[:, None] == key_ids[None, :])[None]
    scores = jnp.where(same_image, scores, -jnp.inf)
    weights_bf = jax.nn.softmax(scores, axis=-1).astype(jnp.bfloat16)
    heads_out = jnp.einsum(
        "hqk,khd->qhd", weights_bf, value_block, preferred_element_type=jnp.float32
    )
    heads_out = heads_out.astype(jnp.bfloat16).reshape(tok_rows, col_width)
    out_full = lax.all_gather(w_out, "seq", axis=0, tiled=True)
    attended = jnp.dot(
        lax.all_gather(heads_out, "tensor", axis=1, tiled=True),
        out_full,
        preferred_element_type=jnp.float32,
    )
    return attended.astype(jnp.bfloat16)


def solution(mesh):
    in_specs = (
        P("seq", "tensor"),
        P(),
        P("seq", "tensor"),
        P("seq", "tensor"),
        P("seq", "tensor"),
        P("seq", "tensor"),
    )
    out_specs = P("seq", "tensor")
    return jax.shard_map(
        on_device, mesh=mesh, in_specs=in_specs, out_specs=out_specs, check_vma=False
    )
```

profile of v0, /device:TPU:0, one launch (start us, length us, event | category | flops | bytes accessed | tf_op | source)
XLA Modules:
  0.0 243.4 jit_solution(93550354333636955)
XLA Ops:
  6.5 0.0 all-gather.6.cloned.1.call-start
  6.5 0.7 all-gather.6.cloned.1.call-update
  7.3 0.0 all-gather.8.cloned.1.call-start
  7.3 0.7 all-gather.8.cloned.1.call-update
  8.0 0.0 all-gather.10.cloned.1.call-start
  8.1 0.7 all-gather.10.cloned.1.call-update
  8.7 0.0 all-gather.12.cloned.1.call-start
  8.8 0.5 all-gather.12.cloned.1.call-update
  9.3 0.0 all-gather.14.cloned.1.call-start
  9.4 0.5 all-gather.14.cloned.1.call-update
  10.0 0.8 constant_dynamic-update-slice_fusion.7
  10.8 0.8 constant_dynamic-update-slice_fusion.20
  11.5 0.8 constant_dynamic-update-slice_fusion.19
  12.3 0.8 constant_dynamic-update-slice_fusion.18
  13.1 0.8 constant_dynamic-update-slice_fusion.17
  13.8 0.8 constant_dynamic-update-slice_fusion.16
  14.6 0.8 constant_dynamic-update-slice_fusion.15
  15.4 1.1 broadcast_compare_fusion
  16.4 58.7 %all-gather.6.cloned.1.call-done = bf16[256,6144]{1,0:T(8,128)(2,1)} async-done(((bf16[256,1536]{1,0:T(8,128)(2,1)}), bf16[256,6144]{1,0:T(8,128)(2,1)}) %all-gather.6.cloned.1.call-update) | async-done | bytes 3145744 | tf_op jit(solution)/shard_map/all_gather | solution.py:22
  75.1 0.0 copy-start
  75.1 32.7 %all-gather.8.cloned.1.call-done = bf16[6144,256]{1,0:T(8,128)(2,1)} async-done(((bf16[768,256]{1,0:T(8,128)(2,1)}), bf16[6144,256]{1,0:T(8,128)(2,1)}) %all-gather.8.cloned.1.call-update) | async-done | bytes 3145744 | tf_op jit(solution)/shard_map/all_gather | solution.py:26
  107.8 4.2 %convolution_convert_fusion.3 = bf16[256,256]{0,1:T(8,128)(2,1)S(1)} fusion(bf16[256,6144]{1,0:T(8,128)(2,1)} %all-gather.6.cloned.1.call-done, bf16[6144,256]{1,0:T(8,128)(2,1)} %all-gather.8.cloned.1.call-done), kind=kOutput, calls=%fused_computation.10 | convolution fusion | flops 805371904 | bytes 6422528 | tf_op jit(solution)/shard_map/dot_general | solution.py:28
  112.0 1.3 collective-permute-start.5
  113.3 1.3 collective-permute-start.4
  114.6 1.3 collective-permute-start.3
  115.9 5.8 %collective-permute-start.1 = (bf16[256,2,128]{0,2,1:T(8,128)(2,1)S(1)}, bf16[256,2,128]{0,2,1:T(8,128)(2,1)}, u32[]{:S(2)}, u32[]{:S(2)}) collective-permute-start(bf16[256,2,128]{0,2,1:T(8,128)(2,1)S(1)} %bitcast.22), channel_id=1, source_target_pairs={{0,8},{4,12},{8,16},{12,20},{16,24},{20,28},{1,9},{5,13},{9,17},{1... | collective-permute-start | bytes 393224 | tf_op jit(solution)/shard_map/ppermute | solution.py:13
  121.8 3.0 %collective-permute-start = (bf16[256,2,128]{0,2,1:T(8,128)(2,1)S(1)}, bf16[256,2,128]{0,2,1:T(8,128)(2,1)}, u32[]{:S(2)}, u32[]{:S(2)}) collective-permute-start(bf16[256,2,128]{0,2,1:T(8,128)(2,1)S(1)} %bitcast.23), channel_id=1, source_target_pairs={{0,4},{4,8},{8,12},{12,16},{16,20},{20,24},{24,28},{1,5},{5,9},{9,... | collective-permute-start | bytes 393224 | tf_op jit(solution)/shard_map/ppermute | solution.py:13
  124.8 21.1 %all-gather.10.cloned.1.call-done = bf16[6144,256]{1,0:T(8,128)(2,1)} async-done(((bf16[768,256]{1,0:T(8,128)(2,1)}), bf16[6144,256]{1,0:T(8,128)(2,1)}) %all-gather.10.cloned.1.call-update) | async-done | bytes 3145744 | tf_op jit(solution)/shard_map/all_gather | solution.py:24
  145.9 0.0 copy-done
  145.9 3.2 %convolution_convert_fusion.2 = bf16[256,256]{0,1:T(8,128)(2,1)S(1)} fusion(bf16[256,6144]{1,0:T(8,128)(2,1)S(1)} %copy-done, bf16[6144,256]{1,0:T(8,128)(2,1)} %all-gather.10.cloned.1.call-done), kind=kOutput, calls=%fused_computation.9 | convolution fusion | flops 805371904 | bytes 6422528 | tf_op jit(solution)/shard_map/dot_general | solution.py:28
  149.1 30.7 %all-gather.12.cloned.1.call-done = bf16[6144,256]{1,0:T(8,128)(2,1)} async-done(((bf16[768,256]{1,0:T(8,128)(2,1)}), bf16[6144,256]{1,0:T(8,128)(2,1)}) %all-gather.12.cloned.1.call-update) | async-done | bytes 3145744 | tf_op jit(solution)/shard_map/all_gather | solution.py:25
  179.9 3.2 %convolution_convert_fusion.1 = bf16[256,256]{0,1:T(8,128)(2,1)S(1)} fusion(bf16[256,6144]{1,0:T(8,128)(2,1)S(1)} %copy-done, bf16[6144,256]{1,0:T(8,128)(2,1)} %all-gather.12.cloned.1.call-done), kind=kOutput, calls=%fused_computation.8 | convolution fusion | flops 805371904 | bytes 6422528 | tf_op jit(solution)/shard_map/dot_general | solution.py:28
  183.1 0.0 copy-start.1
  183.1 0.1 copy.13
  183.3 0.0 collective-permute-done
  183.3 3.2 %collective-permute-start.2 = (bf16[256,2,128]{0,2,1:T(8,128)(2,1)S(1)}, bf16[256,2,128]{0,2,1:T(8,128)(2,1)S(1)}, u32[]{:S(2)}, u32[]{:S(2)}) collective-permute-start(bf16[256,2,128]{0,2,1:T(8,128)(2,1)S(1)} %bitcast.25), channel_id=1, source_target_pairs={{0,12},{4,16},{8,20},{12,24},{16,28},{1,13},{5,17},{9,21},{13,25},... | collective-permute-start | bytes 393224 | tf_op jit(solution)/shard_map/ppermute | solution.py:13
  186.5 0.9 constant_dynamic-update-slice_fusion.5
  187.4 0.0 collective-permute-done.1
  187.4 1.3 collective-permute-start.11
  188.7 0.9 constant_dynamic-update-slice_fusion.4
  189.7 0.0 collective-permute-done.2
  189.7 1.3 collective-permute-start.10
  191.0 0.0 collective-permute-done.3
  191.0 1.3 collective-permute-start.9
  192.3 0.9 constant_dynamic-update-slice_fusion.2
  193.2 0.0 collective-permute-done.4
  193.2 3.0 %collective-permute-start.6 = (bf16[256,2,128]{2,0,1:T(8,128)(2,1)S(1)}, bf16[256,2,128]{2,0,1:T(8,128)(2,1)S(1)}, u32[]{:S(2)}, u32[]{:S(2)}) collective-permute-start(bf16[256,2,128]{2,0,1:T(8,128)(2,1)S(1)} %copy.13), channel_id=1, source_target_pairs={{0,4},{4,8},{8,12},{12,16},{16,20},{20,24},{24,28},{1,5},{5,9},{9,... | collective-permute-start | bytes 393224 | tf_op jit(solution)/shard_map/ppermute | solution.py:13
  196.3 0.9 constant_dynamic-update-slice_fusion.1
  197.2 0.0 collective-permute-done.5
  197.2 4.8 %collective-permute-start.7 = (bf16[256,2,128]{2,0,1:T(8,128)(2,1)S(1)}, bf16[256,2,128]{2,0,1:T(8,128)(2,1)S(1)}, u32[]{:S(2)}, u32[]{:S(2)}) collective-permute-start(bf16[256,2,128]{2,0,1:T(8,128)(2,1)S(1)} %copy.13), channel_id=1, source_target_pairs={{0,8},{4,12},{8,16},{12,20},{16,24},{20,28},{1,9},{5,13},{9,17},{1... | collective-permute-start | bytes 393224 | tf_op jit(solution)/shard_map/ppermute | solution.py:13
  202.0 0.9 constant_dynamic-update-slice_fusion
  202.9 0.0 collective-permute-done.6
  202.9 5.6 %collective-permute-start.8 = (bf16[256,2,128]{2,0,1:T(8,128)(2,1)S(1)}, bf16[256,2,128]{2,0,1:T(8,128)(2,1)S(1)}, u32[]{:S(2)}, u32[]{:S(2)}) collective-permute-start(bf16[256,2,128]{2,0,1:T(8,128)(2,1)S(1)} %copy.13), channel_id=1, source_target_pairs={{0,12},{4,16},{8,20},{12,24},{16,28},{1,13},{5,17},{9,21},{13,25},... | collective-permute-start | bytes 393224 | tf_op jit(solution)/shard_map/ppermute | solution.py:13
  208.6 0.0 collective-permute-done.7
  208.6 5.1 %collective-permute-done.8 = bf16[256,2,128]{2,0,1:T(8,128)(2,1)S(1)} collective-permute-done((bf16[256,2,128]{2,0,1:T(8,128)(2,1)S(1)}, bf16[256,2,128]{2,0,1:T(8,128)(2,1)S(1)}, u32[]{:S(2)}, u32[]{:S(2)}) %collective-permute-start.8) | collective-permute-done | bytes 131104 | tf_op jit(solution)/shard_map/ppermute | solution.py:13
  213.8 0.0 collective-permute-done.9
  213.8 0.0 collective-permute-done.10
  213.9 0.0 collective-permute-done.11
  213.9 0.0 copy-done.1
  213.9 1.5 exponential_reduce_fusion
  215.4 1.9 fusion.3
  217.3 15.7 %all_gather.22 = bf16[256,1024]{0,1:T(8,128)(2,1)S(1)} all-gather(bf16[256,256]{0,1:T(8,128)(2,1)S(1)} %bitcast.29), channel_id=1, replica_groups=mesh['seq'=8,'tensor'=4] {'tensor'}, dimensions={1}, use_global_device_ids=true | all-gather | bytes 655360 | tf_op jit(solution)/shard_map/all_gather | solution.py:62
  233.1 0.0 all-gather.14.cloned.1.call-done
  233.1 3.8 %convolution_convert_fusion = bf16[256,1536]{1,0:T(8,128)(2,1)} fusion(bf16[256,1024]{0,1:T(8,128)(2,1)S(1)} %all_gather.22, bf16[1024,1536]{1,0:T(8,128)(2,1)} %all-gather.14.cloned.1.call-done), kind=kOutput, calls=%fused_computation.5 | convolution fusion | flops 805699584 | bytes 4456448 | tf_op jit(solution)/shard_map/dot_general | solution.py:61
  (10 shorter events, 0.2 us)
Async XLA Ops:
  6.5 68.6 %all-gather.6.cloned.1.call-start = ((), (), s32[]{:S(2)}) async-start(), calls=%async_computation | async-start | bytes 3932160 | tf_op jit(solution)/shard_map/all_gather | solution.py:22
  7.3 100.6 %all-gather.8.cloned.1.call-start = ((), (), s32[]{:S(2)}) async-start(), calls=%async_computation.1 | async-start | bytes 3538944 | tf_op jit(solution)/shard_map/all_gather | solution.py:26
  8.0 137.9 %all-gather.10.cloned.1.call-start = ((), (), s32[]{:S(2)}) async-start(), calls=%async_computation.2 | async-start | bytes 3538944 | tf_op jit(solution)/shard_map/all_gather | solution.py:24
  8.7 171.1 %all-gather.12.cloned.1.call-start = ((), (), s32[]{:S(2)}) async-start(), calls=%async_computation.3 | async-start | bytes 3538944 | tf_op jit(solution)/shard_map/all_gather | solution.py:25
  9.3 223.8 %all-gather.14.cloned.1.call-start = ((), (), s32[]{:S(2)}) async-start(), calls=%async_computation.4 | async-start | bytes 3538944 | tf_op jit(solution)/shard_map/all_gather | solution.py:60
  75.1 70.8 %copy-start = (bf16[256,6144]{1,0:T(8,128)(2,1)S(1)}, bf16[256,6144]{1,0:T(8,128)(2,1)}, u32[]{:S(2)}) copy-start(bf16[256,6144]{1,0:T(8,128)(2,1)} %all-gather.6.cloned.1.call-done) | copy-start | bytes 9437188
  112.0 85.2 %collective-permute-start.5 = (bf16[256,2,128]{0,2,1:T(8,128)(2,1)S(1)}, bf16[256,2,128]{0,2,1:T(8,128)(2,1)}, u32[]{:S(2)}, u32[]{:S(2)}) collective-permute-start(bf16[256,2,128]{0,2,1:T(8,128)(2,1)S(1)} %bitcast.19), channel_id=1, source_target_pairs={{12,0},{16,4},{20,8},{24,12},{28,16},{13,1},{17,5},{21,9},{25,13},... | collective-permute-start | bytes 393224 | tf_op jit(solution)/shard_map/ppermute | solution.py:13
  113.3 79.9 %collective-permute-start.4 = (bf16[256,2,128]{0,2,1:T(8,128)(2,1)S(1)}, bf16[256,2,128]{0,2,1:T(8,128)(2,1)}, u32[]{:S(2)}, u32[]{:S(2)}) collective-permute-start(bf16[256,2,128]{0,2,1:T(8,128)(2,1)S(1)} %bitcast.20), channel_id=1, source_target_pairs={{8,0},{12,4},{16,8},{20,12},{24,16},{28,20},{9,1},{13,5},{17,9},{2... | collective-permute-start | bytes 393224 | tf_op jit(solution)/shard_map/ppermute | solution.py:13
  114.6 76.4 %collective-permute-start.3 = (bf16[256,2,128]{0,2,1:T(8,128)(2,1)S(1)}, bf16[256,2,128]{0,2,1:T(8,128)(2,1)}, u32[]{:S(2)}, u32[]{:S(2)}) collective-permute-start(bf16[256,2,128]{0,2,1:T(8,128)(2,1)S(1)} %bitcast.21), channel_id=1, source_target_pairs={{4,0},{8,4},{12,8},{16,12},{20,16},{24,20},{28,24},{5,1},{9,5},{13... | collective-permute-start | bytes 393224 | tf_op jit(solution)/shard_map/ppermute | solution.py:13
  115.9 71.5 %collective-permute-start.1 = (bf16[256,2,128]{0,2,1:T(8,128)(2,1)S(1)}, bf16[256,2,128]{0,2,1:T(8,128)(2,1)}, u32[]{:S(2)}, u32[]{:S(2)}) collective-permute-start(bf16[256,2,128]{0,2,1:T(8,128)(2,1)S(1)} %bitcast.22), channel_id=1, source_target_pairs={{0,8},{4,12},{8,16},{12,20},{16,24},{20,28},{1,9},{5,13},{9,17},{1... | collective-permute-start | bytes 393224 | tf_op jit(solution)/shard_map/ppermute | solution.py:13
  121.8 61.5 %collective-permute-start = (bf16[256,2,128]{0,2,1:T(8,128)(2,1)S(1)}, bf16[256,2,128]{0,2,1:T(8,128)(2,1)}, u32[]{:S(2)}, u32[]{:S(2)}) collective-permute-start(bf16[256,2,128]{0,2,1:T(8,128)(2,1)S(1)} %bitcast.23), channel_id=1, source_target_pairs={{0,4},{4,8},{8,12},{12,16},{16,20},{20,24},{24,28},{1,5},{5,9},{9,... | collective-permute-start | bytes 393224 | tf_op jit(solution)/shard_map/ppermute | solution.py:13
  183.1 30.8 %copy-start.1 = (pred[256,1792]{1,0:T(8,128)(4,1)S(1)}, pred[256,1792]{1,0:T(8,128)(4,1)}, u32[]{:S(2)}) copy-start(pred[256,1792]{1,0:T(8,128)(4,1)} %broadcast_compare_fusion) | copy-start | bytes 1376260
  183.3 6.4 %collective-permute-start.2 = (bf16[256,2,128]{0,2,1:T(8,128)(2,1)S(1)}, bf16[256,2,128]{0,2,1:T(8,128)(2,1)S(1)}, u32[]{:S(2)}, u32[]{:S(2)}) collective-permute-start(bf16[256,2,128]{0,2,1:T(8,128)(2,1)S(1)} %bitcast.25), channel_id=1, source_target_pairs={{0,12},{4,16},{8,20},{12,24},{16,28},{1,13},{5,17},{9,21},{13,25},... | collective-permute-start | bytes 393224 | tf_op jit(solution)/shard_map/ppermute | solution.py:13
  187.4 26.4 %collective-permute-start.11 = (bf16[256,2,128]{2,0,1:T(8,128)(2,1)S(1)}, bf16[256,2,128]{2,0,1:T(8,128)(2,1)S(1)}, u32[]{:S(2)}, u32[]{:S(2)}) collective-permute-start(bf16[256,2,128]{2,0,1:T(8,128)(2,1)S(1)} %copy.13), channel_id=1, source_target_pairs={{12,0},{16,4},{20,8},{24,12},{28,16},{13,1},{17,5},{21,9},{25,13},... | collective-permute-start | bytes 393224 | tf_op jit(solution)/shard_map/ppermute | solution.py:13
  189.7 24.1 %collective-permute-start.10 = (bf16[256,2,128]{2,0,1:T(8,128)(2,1)S(1)}, bf16[256,2,128]{2,0,1:T(8,128)(2,1)S(1)}, u32[]{:S(2)}, u32[]{:S(2)}) collective-permute-start(bf16[256,2,128]{2,0,1:T(8,128)(2,1)S(1)} %copy.13), channel_id=1, source_target_pairs={{8,0},{12,4},{16,8},{20,12},{24,16},{28,20},{9,1},{13,5},{17,9},{2... | collective-permute-start | bytes 393224 | tf_op jit(solution)/shard_map/ppermute | solution.py:13
  191.0 22.8 %collective-permute-start.9 = (bf16[256,2,128]{2,0,1:T(8,128)(2,1)S(1)}, bf16[256,2,128]{2,0,1:T(8,128)(2,1)S(1)}, u32[]{:S(2)}, u32[]{:S(2)}) collective-permute-start(bf16[256,2,128]{2,0,1:T(8,128)(2,1)S(1)} %copy.13), channel_id=1, source_target_pairs={{4,0},{8,4},{12,8},{16,12},{20,16},{24,20},{28,24},{5,1},{9,5},{13... | collective-permute-start | bytes 393224 | tf_op jit(solution)/shard_map/ppermute | solution.py:13
  193.2 9.7 %collective-permute-start.6 = (bf16[256,2,128]{2,0,1:T(8,128)(2,1)S(1)}, bf16[256,2,128]{2,0,1:T(8,128)(2,1)S(1)}, u32[]{:S(2)}, u32[]{:S(2)}) collective-permute-start(bf16[256,2,128]{2,0,1:T(8,128)(2,1)S(1)} %copy.13), channel_id=1, source_target_pairs={{0,4},{4,8},{8,12},{12,16},{16,20},{20,24},{24,28},{1,5},{5,9},{9,... | collective-permute-start | bytes 393224 | tf_op jit(solution)/shard_map/ppermute | solution.py:13
  197.2 11.4 %collective-permute-start.7 = (bf16[256,2,128]{2,0,1:T(8,128)(2,1)S(1)}, bf16[256,2,128]{2,0,1:T(8,128)(2,1)S(1)}, u32[]{:S(2)}, u32[]{:S(2)}) collective-permute-start(bf16[256,2,128]{2,0,1:T(8,128)(2,1)S(1)} %copy.13), channel_id=1, source_target_pairs={{0,8},{4,12},{8,16},{12,20},{16,24},{20,28},{1,9},{5,13},{9,17},{1... | collective-permute-start | bytes 393224 | tf_op jit(solution)/shard_map/ppermute | solution.py:13
  202.9 10.8 %collective-permute-start.8 = (bf16[256,2,128]{2,0,1:T(8,128)(2,1)S(1)}, bf16[256,2,128]{2,0,1:T(8,128)(2,1)S(1)}, u32[]{:S(2)}, u32[]{:S(2)}) collective-permute-start(bf16[256,2,128]{2,0,1:T(8,128)(2,1)S(1)} %copy.13), channel_id=1, source_target_pairs={{0,12},{4,16},{8,20},{12,24},{16,28},{1,13},{5,17},{9,21},{13,25},... | collective-permute-start | bytes 393224 | tf_op jit(solution)/shard_map/ppermute | solution.py:13
Sparse Core Ops, SparseCore 0:
  8.9 66.1 all-gather.5
  77.0 30.8 all-gather.7
  109.7 36.1 all-gather.9
  147.6 32.1 all-gather.11
  181.6 40.0 all-gather.13
where the time goes:
time: 244 us; the launch traced here: 243 us
  waiting for transfers between devices  152 us (62%)
  starting transfers between devices  33.4 us (14%)
  matrix products  17.8 us (7%)
  blocking collectives  15.7 us (6%)
  between operations  13.5 us (6%)
  other arithmetic  6.45 us (3%)
  local copies, waits for them, and re-layouts  4.87 us (2%)
    all_gather x1, waiting for transfers between devices, on_device(): gathered = lax.all_gather(patches, 'tensor', axis=1, tiled=True)  58.7 us
    ppermute x12, starting transfers between devices, shifted(): return lax.ppermute(x, axis, pairs)  33.3 us
    all_gather x1, waiting for transfers between devices, on_device(): lax.all_gather(w_value, 'seq', axis=0, tiled=True)  32.7 us
    all_gather x1, waiting for transfers between devices, on_device(): lax.all_gather(w_key, 'seq', axis=0, tiled=True)  30.7 us
    all_gather x1, waiting for transfers between devices, on_device(): lax.all_gather(w_query, 'seq', axis=0, tiled=True)  21.1 us
    all_gather x1, blocking collectives, on_device(): lax.all_gather(heads_out, 'tensor', axis=1, tiled=True)  15.7 us
    dot_general x3, matrix products, on_device(): jnp.dot(gathered, piece, preferred_element_type=jnp.float32)  10.6 us
    ppermute x12, waiting for transfers between devices, shifted(): return lax.ppermute(x, axis, pairs)  5.16 us
  transfers between devices with their start and end apart: 17, of which 5 were waited for; matrix products, arithmetic and copies ran while one was open for 10% of the time, Pallas kernels for 0%

commit v1 on v0

--- a/solution.py
+++ b/solution.py
@@ -19,7 +19,14 @@
     local_heads = col_width // HS
     seq_count = lax.axis_size("seq")
     device = lax.axis_index("seq")
-    gathered = lax.all_gather(patches, "tensor", axis=1, tiled=True)
+    ring = [patches]
+    for hop in range(3):
+        ring.append(lax.ppermute(ring[-1], "tensor", [(dev, (dev + 1) % 4) for dev in range(4)]))
+    gathered = jnp.roll(
+        jnp.concatenate(ring[::-1], axis=1),
+        (lax.axis_index("tensor") + 1) * ring[0].shape[1],
+        axis=1,
+    )
     pieces = (
         lax.all_gather(w_query, "seq", axis=0, tiled=True),
         lax.all_gather(w_key, "seq", axis=0, tiled=True),

time: 244 us -> 178 us (0.73)
  waiting for transfers between devices: 152 us -> 79.8 us
  matrix products: 17.8 us -> 21.9 us
  local copies, waits for them, and re-layouts: 4.87 us -> 8.31 us
    all_gather x1 -> x0, waiting for transfers between devices: 58.7 us -> none  [on_device(): gathered = lax.all_gather(patches, 'tensor', axis=1, tiled=True)]
    ppermute x0 -> x3, waiting for transfers between devices: none -> 53.4 us  [on_device(): lax.ppermute(ring[-1], 'tensor', [(dev, (dev + 1) % 4) for dev in range(4)])]
    all_gather x1, waiting for transfers between devices: 30.7 us -> 0.01 us  [on_device(): lax.all_gather(w_key, 'seq', axis=0, tiled=True)]
    all_gather x1, waiting for transfers between devices: 21.1 us -> 0.02 us  [on_device(): lax.all_gather(w_query, 'seq', axis=0, tiled=True)]
    all_gather x1, waiting for transfers between devices: 32.7 us -> 14.8 us  [on_device(): lax.all_gather(w_value, 'seq', axis=0, tiled=True)]
    ppermute x12, starting transfers between devices: 33.3 us -> 27.7 us  [shifted(): return lax.ppermute(x, axis, pairs)]
    ppermute x12, waiting for transfers between devices: 5.16 us -> 9.53 us  [shifted(): return lax.ppermute(x, axis, pairs)]
    dot_general x3, matrix products: 10.6 us -> 14.7 us  [on_device(): jnp.dot(gathered, piece, preferred_element_type=jnp.float32)]
  transfers between devices with their start and end apart: 17 -> 19, of which waited for: 5 -> 6; matrix products, arithmetic and copies ran while one was open for 10% -> 19% of each run, Pallas kernels for 0% -> 0%
where the time goes in v1:
time: 178 us; the launch traced here: 177 us
  waiting for transfers between devices  79.8 us (45%)
  starting transfers between devices  31 us (17%)
  matrix products  21.9 us (12%)
  blocking collectives  16 us (9%)
  between operations  13.5 us (8%)
  local copies, waits for them, and re-layouts  8.31 us (5%)
  other arithmetic  6.47 us (4%)
    ppermute x3, waiting for transfers between devices, on_device(): lax.ppermute(ring[-1], 'tensor', [(dev, (dev + 1) % 4) for dev in range(4)])  53.4 us
    ppermute x12, starting transfers between devices, shifted(): return lax.ppermute(x, axis, pairs)  27.7 us
    all_gather x1, blocking collectives, on_device(): lax.all_gather(heads_out, 'tensor', axis=1, tiled=True)  16 us
    all_gather x1, waiting for transfers between devices, on_device(): lax.all_gather(w_value, 'seq', axis=0, tiled=True)  14.8 us
    dot_general x3, matrix products, on_device(): jnp.dot(gathered, piece, preferred_element_type=jnp.float32)  14.7 us
    ppermute x12, waiting for transfers between devices, shifted(): return lax.ppermute(x, axis, pairs)  9.53 us
    unnamed x23, local copies, waits for them, and re-layouts  7.16 us
    unnamed x7, other arithmetic  4.61 us
  transfers between devices with their start and end apart: 19, of which 6 were waited for; matrix products, arithmetic and copies ran while one was open for 19% of the time, Pallas kernels for 0%

profile of v1, /device:TPU:0, one launch (start us, length us, event | category | flops | bytes accessed | tf_op | source)
XLA Modules:
  0.0 177.0 jit_solution(5426305804534415237)
XLA Ops:
  6.5 0.7 all-gather.9.cloned.1.call-update
  7.3 0.0 all-gather.7.cloned.1.call-start
  7.3 0.7 all-gather.7.cloned.1.call-update
  8.0 0.0 all-gather.5.cloned.1.call-start
  8.1 0.7 all-gather.5.cloned.1.call-update
  8.7 0.0 all-gather.11.cloned.1.call-start
  8.8 3.1 %collective-permute-start = (bf16[256,1536]{1,0:T(8,128)(2,1)}, bf16[256,1536]{1,0:T(8,128)(2,1)S(1)}, u32[]{:S(2)}, u32[]{:S(2)}) collective-permute-start(bf16[256,1536]{1,0:T(8,128)(2,1)} %param.6), channel_id=1, source_target_pairs={{0,1},{1,2},{2,3},{3,0},{4,5},{5,6},{6,7},{7,4},{8,9},{9,10},{10,1... | collective-permute-start | bytes 2359304 | tf_op jit(solution)/shard_map/ppermute | solution.py:24
  11.9 19.8 %collective-permute-done = bf16[256,1536]{1,0:T(8,128)(2,1)S(1)} collective-permute-done((bf16[256,1536]{1,0:T(8,128)(2,1)}, bf16[256,1536]{1,0:T(8,128)(2,1)S(1)}, u32[]{:S(2)}, u32[]{:S(2)}) %collective-permute-start) | collective-permute-done | bytes 786464 | tf_op jit(solution)/shard_map/ppermute | solution.py:24
  31.7 0.0 collective-permute-start.1
  31.7 0.0 all-gather.11.cloned.1.call-update
  31.8 0.8 constant_dynamic-update-slice_fusion.15
  32.5 0.8 constant_dynamic-update-slice_fusion.28
  33.3 0.8 constant_dynamic-update-slice_fusion.27
  34.1 0.8 constant_dynamic-update-slice_fusion.26
  34.8 17.3 %collective-permute-done.1 = bf16[256,1536]{1,0:T(8,128)(2,1)S(1)} collective-permute-done((bf16[256,1536]{1,0:T(8,128)(2,1)S(1)}, bf16[256,1536]{1,0:T(8,128)(2,1)S(1)}, u32[]{:S(2)}, u32[]{:S(2)}) %collective-permute-start.1) | collective-permute-done | bytes 786464 | tf_op jit(solution)/shard_map/ppermute | solution.py:24
  52.2 0.0 collective-permute-start.2
  52.2 0.8 constant_dynamic-update-slice_fusion.25
  52.9 0.8 constant_dynamic-update-slice_fusion.24
  53.7 0.8 constant_dynamic-update-slice_fusion.23
  54.5 1.1 broadcast_compare_fusion
  55.6 16.2 %collective-permute-done.2 = bf16[256,1536]{1,0:T(8,128)(2,1)S(1)} collective-permute-done((bf16[256,1536]{1,0:T(8,128)(2,1)S(1)}, bf16[256,1536]{1,0:T(8,128)(2,1)S(1)}, u32[]{:S(2)}, u32[]{:S(2)}) %collective-permute-start.2) | collective-permute-done | bytes 786464 | tf_op jit(solution)/shard_map/ppermute | solution.py:24
  71.8 1.0 constant_dynamic-update-slice_fusion.7
  72.8 1.0 constant_dynamic-update-slice_fusion.6
  73.8 1.0 constant_dynamic-update-slice_fusion.5
  74.8 1.0 constant_dynamic-update-slice_fusion.4
  75.7 1.0 constant_dynamic-update-slice_fusion.3
  76.7 1.0 constant_dynamic-update-slice_fusion.2
  77.7 1.1 constant_dynamic-update-slice_fusion.1
  78.8 1.0 constant_dynamic-update-slice_fusion
  79.8 4.9 %fusion.15 = bf16[256,256]{0,1:T(8,128)(2,1)S(1)} fusion(bf16[6144,256]{1,0:T(8,128)(2,1)} %all-gather.9.cloned.1.call-done, bf16[256,12288]{1,0:T(8,128)(2,1)} %constant_dynamic-update-slice_fusion, s32[]{:T(128)S(6)} %select_n.86), kind=kOutput, calls=%fused_computation.15 | convolution fusion | flops 805371904 | bytes 6422532 | tf_op jit(solution)/shard_map/dot_general | solution.py:35
  84.7 0.1 copy.13
  84.8 1.3 collective-permute-start.9
  86.1 3.6 %collective-permute-start.10 = (bf16[256,2,128]{2,0,1:T(8,128)(2,1)S(1)}, bf16[256,2,128]{2,0,1:T(8,128)(2,1)S(1)}, u32[]{:S(2)}, u32[]{:S(2)}) collective-permute-start(bf16[256,2,128]{2,0,1:T(8,128)(2,1)S(1)} %copy.13), channel_id=1, source_target_pairs={{0,8},{4,12},{8,16},{12,20},{16,24},{20,28},{1,9},{5,13},{9,17},{1... | collective-permute-start | bytes 393224 | tf_op jit(solution)/shard_map/ppermute | solution.py:13
  89.7 4.3 %collective-permute-start.11 = (bf16[256,2,128]{2,0,1:T(8,128)(2,1)S(1)}, bf16[256,2,128]{2,0,1:T(8,128)(2,1)S(1)}, u32[]{:S(2)}, u32[]{:S(2)}) collective-permute-start(bf16[256,2,128]{2,0,1:T(8,128)(2,1)S(1)} %copy.13), channel_id=1, source_target_pairs={{0,12},{4,16},{8,20},{12,24},{16,28},{1,13},{5,17},{9,21},{13,25},... | collective-permute-start | bytes 393224 | tf_op jit(solution)/shard_map/ppermute | solution.py:13
  94.1 1.3 collective-permute-start.12
  95.4 1.3 collective-permute-start.13
  96.7 0.0 all-gather.7.cloned.1.call-done
  96.7 4.9 %fusion.12 = bf16[256,256]{0,1:T(8,128)(2,1)S(1)} fusion(bf16[6144,256]{1,0:T(8,128)(2,1)} %all-gather.7.cloned.1.call-done, bf16[256,12288]{1,0:T(8,128)(2,1)} %constant_dynamic-update-slice_fusion, s32[]{:T(128)S(6)} %select_n.86), kind=kOutput, calls=%fused_computation.14 | convolution fusion | flops 805371904 | bytes 6422532 | tf_op jit(solution)/shard_map/dot_general | solution.py:35
  101.6 0.0 copy-start.1
  101.6 14.8 %all-gather.5.cloned.1.call-done = bf16[6144,256]{1,0:T(8,128)(2,1)} async-done(((bf16[768,256]{1,0:T(8,128)(2,1)}), bf16[6144,256]{1,0:T(8,128)(2,1)}) %all-gather.5.cloned.1.call-update) | async-done | bytes 3145744 | tf_op jit(solution)/shard_map/all_gather | solution.py:33
  116.5 4.9 %fusion.9 = bf16[256,256]{0,1:T(8,128)(2,1)S(1)} fusion(bf16[6144,256]{1,0:T(8,128)(2,1)} %all-gather.5.cloned.1.call-done, bf16[256,12288]{1,0:T(8,128)(2,1)} %constant_dynamic-update-slice_fusion, s32[]{:T(128)S(6)} %select_n.86), kind=kOutput, calls=%fused_computation.13 | convolution fusion | flops 805371904 | bytes 6422532 | tf_op jit(solution)/shard_map/dot_general | solution.py:35
  121.4 0.0 collective-permute-done.9
  121.4 1.3 collective-permute-start.14
  122.7 0.0 collective-permute-done.10
  122.7 2.2 %collective-permute-start.3 = (bf16[256,2,128]{0,2,1:T(8,128)(2,1)S(1)}, bf16[256,2,128]{0,2,1:T(8,128)(2,1)S(1)}, u32[]{:S(2)}, u32[]{:S(2)}) collective-permute-start(bf16[256,2,128]{0,2,1:T(8,128)(2,1)S(1)} %bitcast.17), channel_id=1, source_target_pairs={{0,4},{4,8},{8,12},{12,16},{16,20},{20,24},{24,28},{1,5},{5,9},{9,... | collective-permute-start | bytes 393224 | tf_op jit(solution)/shard_map/ppermute | solution.py:13
  124.9 0.0 collective-permute-done.11
  124.9 4.4 %collective-permute-start.4 = (bf16[256,2,128]{0,2,1:T(8,128)(2,1)S(1)}, bf16[256,2,128]{0,2,1:T(8,128)(2,1)S(1)}, u32[]{:S(2)}, u32[]{:S(2)}) collective-permute-start(bf16[256,2,128]{0,2,1:T(8,128)(2,1)S(1)} %bitcast.18), channel_id=1, source_target_pairs={{0,8},{4,12},{8,16},{12,20},{16,24},{20,28},{1,9},{5,13},{9,17},{1... | collective-permute-start | bytes 393224 | tf_op jit(solution)/shard_map/ppermute | solution.py:13
  129.4 0.0 collective-permute-done.12
  129.4 4.0 %collective-permute-start.5 = (bf16[256,2,128]{0,2,1:T(8,128)(2,1)S(1)}, bf16[256,2,128]{0,2,1:T(8,128)(2,1)S(1)}, u32[]{:S(2)}, u32[]{:S(2)}) collective-permute-start(bf16[256,2,128]{0,2,1:T(8,128)(2,1)S(1)} %bitcast.19), channel_id=1, source_target_pairs={{0,12},{4,16},{8,20},{12,24},{16,28},{1,13},{5,17},{9,21},{13,25},... | collective-permute-start | bytes 393224 | tf_op jit(solution)/shard_map/ppermute | solution.py:13
  133.4 0.0 collective-permute-done.13
  133.5 1.3 collective-permute-start.6
  134.8 0.0 collective-permute-done.14
  134.8 1.3 collective-permute-start.7
  136.1 0.0 collective-permute-done.3
  136.1 1.5 collective-permute-start.8
  137.6 0.0 collective-permute-done.4
  137.7 0.0 collective-permute-done.5
  137.7 0.0 collective-permute-done.6
  137.7 5.2 %collective-permute-done.7 = bf16[256,2,128]{0,2,1:T(8,128)(2,1)S(1)} collective-permute-done((bf16[256,2,128]{0,2,1:T(8,128)(2,1)S(1)}, bf16[256,2,128]{0,2,1:T(8,128)(2,1)S(1)}, u32[]{:S(2)}, u32[]{:S(2)}) %collective-permute-start.7) | collective-permute-done | bytes 131104 | tf_op jit(solution)/shard_map/ppermute | solution.py:13
  142.9 4.3 %collective-permute-done.8 = bf16[256,2,128]{0,2,1:T(8,128)(2,1)S(1)} collective-permute-done((bf16[256,2,128]{0,2,1:T(8,128)(2,1)S(1)}, bf16[256,2,128]{0,2,1:T(8,128)(2,1)S(1)}, u32[]{:S(2)}, u32[]{:S(2)}) %collective-permute-start.8) | collective-permute-done | bytes 131104 | tf_op jit(solution)/shard_map/ppermute | solution.py:13
  147.3 1.5 exponential_reduce_fusion
  148.8 1.9 %fusion.18 = bf16[2,128,256]{2,1,0:T(8,128)(2,1)S(1)} fusion(bf16[1792,2,128]{0,2,1:T(8,128)(2,1)S(1)} %constant_dynamic-update-slice_fusion.8, f32[2,256]{1,0:T(2,128)S(1)} %exponential_reduce_fusion, bf16[256,2,128]{0,2,1:T(8,128)(2,1)S(1)} %bitcast.25, bf16[1792,2,128]{2,0,1:T(8,128)(2,1)S(1)} %constant_dynamic-update-slice_fusion.16, ...), kind=kOutput, calls=%fused_computation.16 | convolution fusion | flops 474417408 | bytes 2557952 | tf_op jit(solution)/shard_map/hqk,khd->qhd/dot_general | solution.py:63
  150.7 16.0 %all_gather.18 = bf16[256,1024]{0,1:T(8,128)(2,1)S(1)} all-gather(bf16[256,256]{0,1:T(8,128)(2,1)S(1)} %bitcast.26), channel_id=1, replica_groups=mesh['seq'=8,'tensor'=4] {'tensor'}, dimensions={1}, use_global_device_ids=true | all-gather | bytes 655360 | tf_op jit(solution)/shard_map/all_gather | solution.py:69
  166.7 3.8 %convolution_convert_fusion = bf16[256,1536]{1,0:T(8,128)(2,1)} fusion(bf16[256,1024]{0,1:T(8,128)(2,1)S(1)} %all_gather.18, bf16[1024,1536]{1,0:T(8,128)(2,1)} %all-gather.11.cloned.1.call-done), kind=kOutput, calls=%fused_computation.5 | convolution fusion | flops 805699584 | bytes 4456448 | tf_op jit(solution)/shard_map/dot_general | solution.py:68
  (21 shorter events, 0.2 us)
Async XLA Ops:
  6.5 68.2 %copy-start = (bf16[256,1536]{1,0:T(8,128)(2,1)S(1)}, bf16[256,1536]{1,0:T(8,128)(2,1)}, u32[]{:S(2)}) copy-start(bf16[256,1536]{1,0:T(8,128)(2,1)} %param.6) | copy-start | bytes 2359300
  6.5 73.3 %all-gather.9.cloned.1.call-start = ((), (), s32[]{:S(2)}) async-start(), calls=%async_computation.2 | async-start | bytes 3538944 | tf_op jit(solution)/shard_map/all_gather | solution.py:32
  7.3 89.4 %all-gather.7.cloned.1.call-start = ((), (), s32[]{:S(2)}) async-start(), calls=%async_computation.1 | async-start | bytes 3538944 | tf_op jit(solution)/shard_map/all_gather | solution.py:31
  8.0 108.4 %all-gather.5.cloned.1.call-start = ((), (), s32[]{:S(2)}) async-start(), calls=%async_computation | async-start | bytes 3538944 | tf_op jit(solution)/shard_map/all_gather | solution.py:33
  8.7 157.9 %all-gather.11.cloned.1.call-start = ((), (), s32[]{:S(2)}) async-start(), calls=%async_computation.3 | async-start | bytes 3538944 | tf_op jit(solution)/shard_map/all_gather | solution.py:67
  8.8 22.9 %collective-permute-start = (bf16[256,1536]{1,0:T(8,128)(2,1)}, bf16[256,1536]{1,0:T(8,128)(2,1)S(1)}, u32[]{:S(2)}, u32[]{:S(2)}) collective-permute-start(bf16[256,1536]{1,0:T(8,128)(2,1)} %param.6), channel_id=1, source_target_pairs={{0,1},{1,2},{2,3},{3,0},{4,5},{5,6},{6,7},{7,4},{8,9},{9,10},{10,1... | collective-permute-start | bytes 2359304 | tf_op jit(solution)/shard_map/ppermute | solution.py:24
  31.7 20.5 %collective-permute-start.1 = (bf16[256,1536]{1,0:T(8,128)(2,1)S(1)}, bf16[256,1536]{1,0:T(8,128)(2,1)S(1)}, u32[]{:S(2)}, u32[]{:S(2)}) collective-permute-start(bf16[256,1536]{1,0:T(8,128)(2,1)S(1)} %collective-permute-done), channel_id=1, source_target_pairs={{0,1},{1,2},{2,3},{3,0},{4,5},{5,6},{6,7},{7,4},{8,9},{9,10},{10,1... | collective-permute-start | bytes 2359304 | tf_op jit(solution)/shard_map/ppermute | solution.py:24
  52.2 19.6 %collective-permute-start.2 = (bf16[256,1536]{1,0:T(8,128)(2,1)S(1)}, bf16[256,1536]{1,0:T(8,128)(2,1)S(1)}, u32[]{:S(2)}, u32[]{:S(2)}) collective-permute-start(bf16[256,1536]{1,0:T(8,128)(2,1)S(1)} %collective-permute-done.1), channel_id=1, source_target_pairs={{0,1},{1,2},{2,3},{3,0},{4,5},{5,6},{6,7},{7,4},{8,9},{9,10},{10,1... | collective-permute-start | bytes 2359304 | tf_op jit(solution)/shard_map/ppermute | solution.py:24
  84.8 36.5 %collective-permute-start.9 = (bf16[256,2,128]{2,0,1:T(8,128)(2,1)S(1)}, bf16[256,2,128]{2,0,1:T(8,128)(2,1)S(1)}, u32[]{:S(2)}, u32[]{:S(2)}) collective-permute-start(bf16[256,2,128]{2,0,1:T(8,128)(2,1)S(1)} %copy.13), channel_id=1, source_target_pairs={{0,4},{4,8},{8,12},{12,16},{16,20},{20,24},{24,28},{1,5},{5,9},{9,... | collective-permute-start | bytes 393224 | tf_op jit(solution)/shard_map/ppermute | solution.py:13
  86.1 36.6 %collective-permute-start.10 = (bf16[256,2,128]{2,0,1:T(8,128)(2,1)S(1)}, bf16[256,2,128]{2,0,1:T(8,128)(2,1)S(1)}, u32[]{:S(2)}, u32[]{:S(2)}) collective-permute-start(bf16[256,2,128]{2,0,1:T(8,128)(2,1)S(1)} %copy.13), channel_id=1, source_target_pairs={{0,8},{4,12},{8,16},{12,20},{16,24},{20,28},{1,9},{5,13},{9,17},{1... | collective-permute-start | bytes 393224 | tf_op jit(solution)/shard_map/ppermute | solution.py:13
  89.7 35.2 %collective-permute-start.11 = (bf16[256,2,128]{2,0,1:T(8,128)(2,1)S(1)}, bf16[256,2,128]{2,0,1:T(8,128)(2,1)S(1)}, u32[]{:S(2)}, u32[]{:S(2)}) collective-permute-start(bf16[256,2,128]{2,0,1:T(8,128)(2,1)S(1)} %copy.13), channel_id=1, source_target_pairs={{0,12},{4,16},{8,20},{12,24},{16,28},{1,13},{5,17},{9,21},{13,25},... | collective-permute-start | bytes 393224 | tf_op jit(solution)/shard_map/ppermute | solution.py:13
  94.1 35.3 %collective-permute-start.12 = (bf16[256,2,128]{2,0,1:T(8,128)(2,1)S(1)}, bf16[256,2,128]{2,0,1:T(8,128)(2,1)S(1)}, u32[]{:S(2)}, u32[]{:S(2)}) collective-permute-start(bf16[256,2,128]{2,0,1:T(8,128)(2,1)S(1)} %copy.13), channel_id=1, source_target_pairs={{4,0},{8,4},{12,8},{16,12},{20,16},{24,20},{28,24},{5,1},{9,5},{13... | collective-permute-start | bytes 393224 | tf_op jit(solution)/shard_map/ppermute | solution.py:13
  95.4 38.1 %collective-permute-start.13 = (bf16[256,2,128]{2,0,1:T(8,128)(2,1)S(1)}, bf16[256,2,128]{2,0,1:T(8,128)(2,1)S(1)}, u32[]{:S(2)}, u32[]{:S(2)}) collective-permute-start(bf16[256,2,128]{2,0,1:T(8,128)(2,1)S(1)} %copy.13), channel_id=1, source_target_pairs={{8,0},{12,4},{16,8},{20,12},{24,16},{28,20},{9,1},{13,5},{17,9},{2... | collective-permute-start | bytes 393224 | tf_op jit(solution)/shard_map/ppermute | solution.py:13
  101.6 45.6 %copy-start.1 = (pred[256,1792]{1,0:T(8,128)(4,1)S(1)}, pred[256,1792]{1,0:T(8,128)(4,1)}, u32[]{:S(2)}) copy-start(pred[256,1792]{1,0:T(8,128)(4,1)} %broadcast_compare_fusion) | copy-start | bytes 1376260
  121.4 13.4 %collective-permute-start.14 = (bf16[256,2,128]{2,0,1:T(8,128)(2,1)S(1)}, bf16[256,2,128]{2,0,1:T(8,128)(2,1)S(1)}, u32[]{:S(2)}, u32[]{:S(2)}) collective-permute-start(bf16[256,2,128]{2,0,1:T(8,128)(2,1)S(1)} %copy.13), channel_id=1, source_target_pairs={{12,0},{16,4},{20,8},{24,12},{28,16},{13,1},{17,5},{21,9},{25,13},... | collective-permute-start | bytes 393224 | tf_op jit(solution)/shard_map/ppermute | solution.py:13
  122.7 13.4 %collective-permute-start.3 = (bf16[256,2,128]{0,2,1:T(8,128)(2,1)S(1)}, bf16[256,2,128]{0,2,1:T(8,128)(2,1)S(1)}, u32[]{:S(2)}, u32[]{:S(2)}) collective-permute-start(bf16[256,2,128]{0,2,1:T(8,128)(2,1)S(1)} %bitcast.17), channel_id=1, source_target_pairs={{0,4},{4,8},{8,12},{12,16},{16,20},{20,24},{24,28},{1,5},{5,9},{9,... | collective-permute-start | bytes 393224 | tf_op jit(solution)/shard_map/ppermute | solution.py:13
  124.9 12.7 %collective-permute-start.4 = (bf16[256,2,128]{0,2,1:T(8,128)(2,1)S(1)}, bf16[256,2,128]{0,2,1:T(8,128)(2,1)S(1)}, u32[]{:S(2)}, u32[]{:S(2)}) collective-permute-start(bf16[256,2,128]{0,2,1:T(8,128)(2,1)S(1)} %bitcast.18), channel_id=1, source_target_pairs={{0,8},{4,12},{8,16},{12,20},{16,24},{20,28},{1,9},{5,13},{9,17},{1... | collective-permute-start | bytes 393224 | tf_op jit(solution)/shard_map/ppermute | solution.py:13
  129.4 8.3 %collective-permute-start.5 = (bf16[256,2,128]{0,2,1:T(8,128)(2,1)S(1)}, bf16[256,2,128]{0,2,1:T(8,128)(2,1)S(1)}, u32[]{:S(2)}, u32[]{:S(2)}) collective-permute-start(bf16[256,2,128]{0,2,1:T(8,128)(2,1)S(1)} %bitcast.19), channel_id=1, source_target_pairs={{0,12},{4,16},{8,20},{12,24},{16,28},{1,13},{5,17},{9,21},{13,25},... | collective-permute-start | bytes 393224 | tf_op jit(solution)/shard_map/ppermute | solution.py:13
  133.5 4.2 %collective-permute-start.6 = (bf16[256,2,128]{0,2,1:T(8,128)(2,1)S(1)}, bf16[256,2,128]{0,2,1:T(8,128)(2,1)S(1)}, u32[]{:S(2)}, u32[]{:S(2)}) collective-permute-start(bf16[256,2,128]{0,2,1:T(8,128)(2,1)S(1)} %bitcast.20), channel_id=1, source_target_pairs={{4,0},{8,4},{12,8},{16,12},{20,16},{24,20},{28,24},{5,1},{9,5},{13... | collective-permute-start | bytes 393224 | tf_op jit(solution)/shard_map/ppermute | solution.py:13
  134.8 8.1 %collective-permute-start.7 = (bf16[256,2,128]{0,2,1:T(8,128)(2,1)S(1)}, bf16[256,2,128]{0,2,1:T(8,128)(2,1)S(1)}, u32[]{:S(2)}, u32[]{:S(2)}) collective-permute-start(bf16[256,2,128]{0,2,1:T(8,128)(2,1)S(1)} %bitcast.21), channel_id=1, source_target_pairs={{8,0},{12,4},{16,8},{20,12},{24,16},{28,20},{9,1},{13,5},{17,9},{2... | collective-permute-start | bytes 393224 | tf_op jit(solution)/shard_map/ppermute | solution.py:13
  136.1 11.1 %collective-permute-start.8 = (bf16[256,2,128]{0,2,1:T(8,128)(2,1)S(1)}, bf16[256,2,128]{0,2,1:T(8,128)(2,1)S(1)}, u32[]{:S(2)}, u32[]{:S(2)}) collective-permute-start(bf16[256,2,128]{0,2,1:T(8,128)(2,1)S(1)} %bitcast.22), channel_id=1, source_target_pairs={{12,0},{16,4},{20,8},{24,12},{28,16},{13,1},{17,5},{21,9},{25,13},... | collective-permute-start | bytes 393224 | tf_op jit(solution)/shard_map/ppermute | solution.py:13
Sparse Core Ops, SparseCore 0:
  9.2 34.8 all-gather.8
  46.0 32.2 all-gather.6
  80.2 36.1 all-gather.4
  118.2 36.2 all-gather.10
